TPU v7x, 256 devices: a whole 4x4x8 slice. The times are simulated.
256 devices in a mesh: dp: 32 (over z_lo, x, core), tensor: 8 (over y, z_hi).
Axes of the slice: x: 4, y: 4, z: 8 (z_hi: 2, z_lo: 4; z = z_hi * 4 + z_lo), core: 2. Of those that a mesh axis runs over, the one named last changes fastest.
Arguments:
- hidden: bfloat16 [32768, 28672], P('dp', 'tensor'), may hold values from -6 to 6
- out_grad: bfloat16 [32768, 8192], P('dp', 'tensor'), may hold values from -6 to 6
- proj_in: bfloat16 [28672, 64], P('tensor'), may hold values from -0.03125 to 0.03125
- proj_out: bfloat16 [8192, 64], P('tensor'), may hold values from -0.0625 to 0.0625
- owner_ids: int32 [32768, 1], P('dp'), may hold values from 0 to 31; in each aligned block of 1024 rows (0 to 1023, 1024 to 2047, ...) at most 128 rows name the same one
- example_ids: int32 [32768], P('dp'), may hold values from 0 to 127
Outputs:
- kernel: float32 [4096, 4096], P('tensor', 'dp')
Inputs may be any that keep to these rules, and one draw needn't show every extreme that they name: `owner_ids`: among the rows of one index of dp, at most 128 name the same owner, and every draw reaches 128.
All inputs are finite; a program needn't handle non-finite values.
Results may differ from a plain program's by a relative error of at most 0.009.
Values may be sent and summed in bfloat16 or wider, within the bound.
A program may use at most 64 MiB of HBM per device.

v0:
```python
import jax
import jax.numpy as jnp
from jax import lax
from jax.sharding import PartitionSpec as P

EX_DEV = 128


def outer_rows(x_rows, g_rows):
    return (x_rows[:, :, None] * g_rows[:, None, :]).reshape(
        x_rows.shape[0], x_rows.shape[1] * g_rows.shape[1]
    )


def member_dot(member, outer):
    member_half = member.astype(jnp.bfloat16)
    upper = outer.astype(jnp.bfloat16)
    lower = (outer - upper.astype(jnp.float32)).astype(jnp.bfloat16)
    first = jnp.dot(member_half, upper, preferred_element_type=jnp.float32)
    return first + jnp.dot(member_half, lower, preferred_element_type=jnp.float32)


def body(hidden, out_grad, proj_in, proj_out, owner_ids, example_ids):
    tensors = lax.axis_size("tensor")
    trank = lax.axis_index("tensor")
    groups = lax.axis_size("dp")
    width = proj_in.shape[1]
    share = width // tensors
    tok = hidden.shape[0]
    x_part = jnp.dot(hidden, proj_in, preferred_element_type=jnp.float32)
    g_part = jnp.dot(out_grad, proj_out, preferred_element_type=jnp.float32)
    send_rows = lax.psum(jnp.concatenate([x_part, g_part], 1), "tensor")
    x_start = trank * share
    columns = send_rows.shape[1]
    owners = owner_ids[:, 0]
    capacity = 4 * tok // groups
    owner_hot = (owners[:, None] == jnp.arange(groups, dtype=jnp.int32)[None, :]).astype(jnp.int32)
    slot_index = jnp.sum(jnp.cumsum(owner_hot, 0) * owner_hot, 1) - 1
    target = owners * capacity + slot_index
    row_buffer = jnp.zeros((groups * capacity, columns), jnp.float32).at[target].set(send_rows)
    id_buffer = (
        jnp.full((groups * capacity,), -1.0, jnp.float32)
        .at[target]
        .set(example_ids.astype(jnp.float32))
    )
    got_rows, got_ids = (
        lax.all_to_all(
            row_buffer.reshape(groups, capacity, columns),
            "dp",
            split_axis=0,
            concat_axis=0,
            tiled=True,
        ),
        lax.all_to_all(
            id_buffer.reshape(groups, capacity), "dp", split_axis=0, concat_axis=0, tiled=True
        ),
    )
    rows = got_rows.reshape(groups * capacity, columns)
    x_rows = lax.dynamic_slice_in_dim(rows, x_start, share, 1)
    g_rows = rows[:, columns - width :]
    member = (
        got_ids.reshape(1, groups * capacity) == jnp.arange(EX_DEV, dtype=jnp.float32)[:, None]
    ).astype(jnp.float32)
    sums = member_dot(member, outer_rows(x_rows, g_rows))
    counts = jnp.sum(member, 1)
    grads = (sums / jnp.maximum(counts, 1.0)[:, None]).astype(jnp.bfloat16)
    products = (
        lax.dot_general(
            lax.all_gather(grads, "dp", axis=0, tiled=True),
            grads,
            (((1,), (1,)), ((), ())),
            preferred_element_type=jnp.float32,
        )
        / width
    )
    return lax.psum_scatter(products, "tensor", scatter_dimension=0, tiled=True)


def solution(mesh):
    in_specs = (
        P("dp", "tensor"),
        P("dp", "tensor"),
        P("tensor", None),
        P("tensor", None),
        P("dp", None),
        P("dp"),
    )
    out_specs = P("tensor", "dp")
    return jax.shard_map(body, mesh=mesh, in_specs=in_specs, out_specs=out_specs, check_vma=False)
```

profile of v0, /device:TPU:6, one launch (start us, length us, event | category | flops | bytes accessed | tf_op | source)
XLA Modules:
  0.0 376.6 jit_solution(12380154530716794183)
XLA Ops:
  6.5 5.6 %fusion.15 = f32[1024,64]{0,1:T(8,128)S(1)} fusion(bf16[1024,3584]{1,0:T(8,128)(2,1)} %param.6, bf16[3584,64]{0,1:T(8,128)(2,1)} %param.8), kind=kOutput, calls=%fused_computation.33 | convolution fusion | flops 469762048 | bytes 8060928 | tf_op jit(solution)/shard_map/dot_general | solution.py:30
  12.2 0.8 fusion.16
  12.9 0.9 pad_maximum_fusion
  13.8 9.0 %reduce-window.6 = s32[32,8,128]{2,1,0:T(8,128)S(1)} reduce-window(s32[32,8,128]{2,1,0:T(8,128)S(1)} %fusion.12, s32[]{:T(128)} %constant.12.clone.1), window={size=1x1x128 pad=0_0x0_0x127_0}, to_apply=%region_0.0 | reduce-window | flops 4161536 | bytes 262148 | tf_op jit(solution)/shard_map/reduce-window
  22.9 0.1 copy.12
  23.4 4.9 %scatter_custom_fusion = f32[4096]{0:T(1024)} fusion(s32[1024]{0:T(1024)S(1)} %bitcast.45, f32[1024]{0:T(1024)S(1)} %convert_element_type.27, f32[]{:T(128)} %constant.10.clone.1), kind=kCustom, calls=%fused_computation.28 | custom fusion | bytes 16388 | tf_op jit(solution)/shard_map/scatter | solution.py:44
  28.3 9.0 %all-to-all-start = ((f32[32,1,128]{2,1,0:T(1,128)}), f32[32,1,128]{2,1,0:T(1,128)S(1)}, u32[]{:S(2)}, u32[]{:S(2)}) async-start(f32[32,1,128]{2,1,0:T(1,128)} %bitcast.6), calls=%async_computation | async-start | bytes 32768 | tf_op jit(solution)/shard_map/all_to_all | solution.py:54
  37.3 91.8 %all-reduce.2.cloned.1.call-done = f32[1024,128]{0,1:T(8,128)} async-done(((f32[1024,128]{0,1:T(8,128)}), f32[1024,128]{0,1:T(8,128)}) %all-reduce.2.cloned.1.call-update) | async-done | bytes 524304 | tf_op jit(solution)/shard_map/psum | solution.py:32
  129.1 1.2 copy.14
  130.3 4.5 %scatter_custom_fusion.1 = f32[4096,128]{1,0:T(8,128)} fusion(s32[1024]{0:T(1024)S(1)} %bitcast.46, f32[1024,128]{1,0:T(8,128)S(1)} %copy.14, f32[]{:T(128)} %constant.6.clone.1), kind=kCustom, calls=%fused_computation.15 | custom fusion | bytes 2097156 | tf_op jit(solution)/shard_map/scatter | solution.py:40
  134.8 5.0 %all-to-all-start.1 = ((f32[32,128,128]{2,1,0:T(8,128)}), f32[32,128,128]{2,1,0:T(8,128)}, u32[]{:S(2)}, u32[]{:S(2)}) async-start(f32[32,128,128]{2,1,0:T(8,128)} %bitcast.36), calls=%async_computation.1 | async-start | bytes 4194304 | tf_op jit(solution)/shard_map/all_to_all | solution.py:47
  139.8 0.3 convert_reduce_fusion
  140.1 48.2 %all-to-all-done.1 = f32[32,128,128]{2,1,0:T(8,128)} async-done(((f32[32,128,128]{2,1,0:T(8,128)}), f32[32,128,128]{2,1,0:T(8,128)}, u32[]{:S(2)}, u32[]{:S(2)}) %all-to-all-start.1) | async-done | bytes 2097184 | tf_op jit(solution)/shard_map/all_to_all | solution.py:47
  188.3 3.5 slice.14
  191.8 3.5 constant_dynamic-slice_fusion
  195.3 2.2 copy.17
  197.5 2.2 copy.18
  199.7 1.0 broadcast_multiply_fusion
  200.7 4.7 %fusion = (bf16[4096,512]{0,1:T(8,128)(2,1)}, bf16[4096,512]{0,1:T(8,128)(2,1)}) fusion(f32[4096,8,64]{0,2,1:T(8,128)S(1)} %broadcast_multiply_fusion), kind=kLoop, calls=%fused_computation.4 | loop fusion | flops 8388608 | bytes 16777216 | tf_op jit(solution)/shard_map/convert_element_type | solution.py:18
  205.4 3.8 %fusion.1 = f32[128,512]{1,0:T(8,128)S(1)} fusion(bf16[4096,512]{0,1:T(8,128)(2,1)} %get-tuple-element.5, f32[4096]{0:T(1024)S(1)} %bitcast.39), kind=kOutput, calls=%fused_computation.10 | convolution fusion | flops 538443776 | bytes 4472832 | tf_op jit(solution)/shard_map/dot_general | solution.py:20
  209.3 2.2 fusion.5
  211.5 58.5 %all-gather.2.cloned.1.call-done = bf16[4096,512]{1,0:T(8,128)(2,1)} async-done(((bf16[128,512]{1,0:T(8,128)(2,1)}), bf16[4096,512]{1,0:T(8,128)(2,1)}) %all-gather.2.cloned.1.call-update) | async-done | bytes 4194320 | tf_op jit(solution)/shard_map/all_gather | solution.py:69
  270.1 4.8 %convolution_multiply_fusion = f32[4096,128]{1,0:T(8,128)} fusion(bf16[4096,512]{1,0:T(8,128)(2,1)} %all-gather.2.cloned.1.call-done, bf16[128,512]{1,0:T(8,128)(2,1)} %fusion.5), kind=kOutput, calls=%fused_computation.5 | convolution fusion | flops 537395200 | bytes 6422528 | tf_op jit(solution)/shard_map/dot_general | solution.py:68
  274.9 95.2 %reduce-scatter.2.cloned.1.call-done = f32[512,128]{1,0:T(8,128)} async-done(((f32[4096,128]{1,0:T(8,128)}), f32[512,128]{1,0:T(8,128)}) %reduce-scatter.2.cloned.1.call-update) | async-done | bytes 262160 | tf_op jit(solution)/shard_map/reduce_scatter | solution.py:76
  (28 shorter events, 0.5 us)
Async XLA Ops:
  6.5 5.6 %copy-start = (bf16[1024,1024]{1,0:T(8,128)(2,1)S(1)}, bf16[1024,1024]{1,0:T(8,128)(2,1)}, u32[]{:S(2)}) copy-start(bf16[1024,1024]{1,0:T(8,128)(2,1)} %param.7) | copy-start | bytes 6291460
  6.5 5.6 %copy-start.2 = (bf16[1024,64]{0,1:T(8,128)(2,1)S(1)}, bf16[1024,64]{0,1:T(8,128)(2,1)}, u32[]{:S(2)}) copy-start(bf16[1024,64]{0,1:T(8,128)(2,1)} %param.9) | copy-start | bytes 393220
  6.5 122.5 %all-reduce.2.cloned.1.call-start = ((), (), s32[]{:S(2)}) async-start(), calls=%async_computation.3 | async-start | bytes 1048576 | tf_op jit(solution)/shard_map/psum | solution.py:32
  12.1 1.7 copy-start.3
  12.1 11.2 %copy-start.4 = (s32[1024]{0:T(1024)S(1)}, s32[1024]{0:T(1024)}, u32[]{:S(2)}) copy-start(s32[1024]{0:T(1024)} %param.11) | copy-start | bytes 12292
  28.3 106.5 %all-to-all-start = ((f32[32,1,128]{2,1,0:T(1,128)}), f32[32,1,128]{2,1,0:T(1,128)S(1)}, u32[]{:S(2)}, u32[]{:S(2)}) async-start(f32[32,1,128]{2,1,0:T(1,128)} %bitcast.6), calls=%async_computation | async-start | bytes 32768 | tf_op jit(solution)/shard_map/all_to_all | solution.py:54
  134.8 53.5 %all-to-all-start.1 = ((f32[32,128,128]{2,1,0:T(8,128)}), f32[32,128,128]{2,1,0:T(8,128)}, u32[]{:S(2)}, u32[]{:S(2)}) async-start(f32[32,128,128]{2,1,0:T(8,128)} %bitcast.36), calls=%async_computation.1 | async-start | bytes 4194304 | tf_op jit(solution)/shard_map/all_to_all | solution.py:47
  139.8 130.3 %all-gather.2.cloned.1.call-start = ((), (), s32[]{:S(2)}) async-start(), calls=%async_computation.4 | async-start | bytes 4325376 | tf_op jit(solution)/shard_map/all_gather | solution.py:69
  205.4 3.9 %copy-start.1 = (bf16[4096,512]{0,1:T(8,128)(2,1)S(1)}, bf16[4096,512]{0,1:T(8,128)(2,1)}, u32[]{:S(2)}) copy-start(bf16[4096,512]{0,1:T(8,128)(2,1)} %get-tuple-element.6) | copy-start | bytes 12582916
  211.5 158.6 %reduce-scatter.2.cloned.1.call-start = ((), (), s32[]{:S(2)}) async-start(), calls=%async_computation.5 | async-start | bytes 2359296 | tf_op jit(solution)/shard_map/reduce_scatter | solution.py:76
Sparse Core Ops, SparseCore 0:
  13.9 115.0 all-reduce.1
  211.6 58.4 all-gather.1
  275.0 95.0 reduce-scatter.1
where the time goes:
time: 377 us
  waiting for transfers between devices  294 us (78%)
  local copies, waits for them, and re-layouts  22.3 us (6%)
  matrix products  17.1 us (5%)
  other arithmetic  16.1 us (4%)
  starting transfers between devices  14.1 us (4%)
  between operations  13.3 us (4%)
    reduce_scatter x1, waiting for transfers between devices, body(): return lax.psum_scatter(products, 'tensor', scatter_dimension=0, tiled=True)  95.2 us
    psum x1, waiting for transfers between devices, body(): send_rows = lax.psum(jnp.concatenate([x_part, g_part], 1), 'tensor')  91.8 us
    all_gather x1, waiting for transfers between devices, body(): lax.all_gather(grads, 'dp', axis=0, tiled=True)  58.5 us
    all_to_all x1, waiting for transfers between devices, body(): lax.all_to_all(row_buffer.reshape(groups, capacity, columns), 'dp', split...  48.2 us
    another operation x3, other arithmetic  9.15 us
    all_to_all x1, starting transfers between devices, body(): lax.all_to_all(id_buffer.reshape(groups, capacity), 'dp', split_axis=0, c...  8.99 us
  transfers between devices with their start and end apart: 5, of which 4 were waited for; matrix products, arithmetic and copies ran while one was open for 5% of the time, Pallas kernels for 0%

commit v1 on v0

--- a/solution.py
+++ b/solution.py
@@ -29,7 +29,7 @@
     tok = hidden.shape[0]
     x_part = jnp.dot(hidden, proj_in, preferred_element_type=jnp.float32)
     g_part = jnp.dot(out_grad, proj_out, preferred_element_type=jnp.float32)
-    send_rows = lax.psum(jnp.concatenate([x_part, g_part], 1), "tensor")
+    send_rows = jnp.sum(lax.all_gather(jnp.concatenate([x_part, g_part], 1), "tensor"), axis=0)
     x_start = trank * share
     columns = send_rows.shape[1]
     owners = owner_ids[:, 0]

time: 377 us -> 377 us (level)
  waiting for transfers between devices: 294 us -> 288 us
  local copies, waits for them, and re-layouts: 22.3 us -> 26.7 us
    psum x1 -> x0, waiting for transfers between devices: 91.8 us -> none  [body(): send_rows = lax.psum(jnp.concatenate([x_part, g_part], 1), 'tensor')]
    all_gather x0 -> x1, waiting for transfers between devices: none -> 86.7 us  [body(): lax.all_gather(jnp.concatenate([x_part, g_part], 1), 'tensor')]
    unnamed x12 -> x13, local copies, waits for them, and re-layouts: 4.36 us -> 9.8 us
  transfers between devices with their start and end apart: 5 -> 5, of which waited for: 4 -> 4; matrix products, arithmetic and copies ran while one was open for 5% -> 7% of each run, Pallas kernels for 0% -> 0%
where the time goes in v1:
time: 377 us
  waiting for transfers between devices  288 us (76%)
  local copies, waits for them, and re-layouts  26.7 us (7%)
  matrix products  17.1 us (5%)
  other arithmetic  17.1 us (5%)
  starting transfers between devices  14.3 us (4%)
  between operations  13.3 us (4%)
    reduce_scatter x1, waiting for transfers between devices, body(): return lax.psum_scatter(products, 'tensor', scatter_dimension=0, tiled=True)  95.4 us
    all_gather x1, waiting for transfers between devices, body(): lax.all_gather(jnp.concatenate([x_part, g_part], 1), 'tensor')  86.7 us
    all_gather x1, waiting for transfers between devices, body(): lax.all_gather(grads, 'dp', axis=0, tiled=True)  58.1 us
    all_to_all x1, waiting for transfers between devices, body(): lax.all_to_all(row_buffer.reshape(groups, capacity, columns), 'dp', split...  48 us
    unnamed x13, local copies, waits for them, and re-layouts  9.8 us
    another operation x3, other arithmetic  9.15 us
    all_to_all x1, starting transfers between devices, body(): lax.all_to_all(id_buffer.reshape(groups, capacity), 'dp', split_axis=0, c...  9 us
  transfers between devices with their start and end apart: 5, of which 4 were waited for; matrix products, arithmetic and copies ran while one was open for 7% of the time, Pallas kernels for 0%

profile of v1, /device:TPU:6, one launch (start us, length us, event | category | flops | bytes accessed | tf_op | source)
XLA Modules:
  0.0 376.7 jit_solution(4223373167693843852)
XLA Ops:
  6.5 5.6 %fusion.15 = f32[1024,64]{0,1:T(8,128)S(1)} fusion(bf16[1024,3584]{1,0:T(8,128)(2,1)} %param.6, bf16[3584,64]{0,1:T(8,128)(2,1)} %param.8), kind=kOutput, calls=%fused_computation.34 | convolution fusion | flops 469762048 | bytes 8060928 | tf_op jit(solution)/shard_map/dot_general | solution.py:30
  12.1 0.8 fusion.16
  12.9 0.8 pad_maximum_fusion
  13.8 9.0 %reduce-window.6 = s32[32,8,128]{2,1,0:T(8,128)S(1)} reduce-window(s32[32,8,128]{2,1,0:T(8,128)S(1)} %fusion.12, s32[]{:T(128)} %constant.12.clone.1), window={size=1x1x128 pad=0_0x0_0x127_0}, to_apply=%region_0.0 | reduce-window | flops 4161536 | bytes 262148 | tf_op jit(solution)/shard_map/reduce-window
  23.3 4.9 %scatter_custom_fusion = f32[4096]{0:T(1024)} fusion(s32[1024]{0:T(1024)S(1)} %bitcast.51, f32[1024]{0:T(1024)S(1)} %convert_element_type.27, f32[]{:T(128)} %constant.10.clone.1), kind=kCustom, calls=%fused_computation.29 | custom fusion | bytes 16388 | tf_op jit(solution)/shard_map/scatter | solution.py:44
  28.2 9.0 %all-to-all-start = ((f32[32,1,128]{2,1,0:T(1,128)}), f32[32,1,128]{2,1,0:T(1,128)S(1)}, u32[]{:S(2)}, u32[]{:S(2)}) async-start(f32[32,1,128]{2,1,0:T(1,128)} %bitcast.6), calls=%async_computation | async-start | bytes 32768 | tf_op jit(solution)/shard_map/all_to_all | solution.py:54
  37.2 86.7 %all-gather.6.cloned.1.call-done = f32[8192,128]{0,1:T(8,128)} async-done(((f32[1024,128]{0,1:T(8,128)}), f32[8192,128]{0,1:T(8,128)}) %all-gather.6.cloned.1.call-update) | async-done | bytes 4194320 | tf_op jit(solution)/shard_map/all_gather | solution.py:32
  124.0 5.4 %copy.26 = f32[16,8,8,1024]{3,2,1,0:T(8,128)S(1)} copy(f32[16,8,8,1024]{3,1,2,0:T(8,128)} %bitcast.42) | data formatting | bytes 8388608
  129.4 1.0 bitcast_reduce_fusion
  130.6 4.5 %scatter_custom_fusion.1 = f32[4096,128]{1,0:T(8,128)} fusion(s32[1024]{0:T(1024)S(1)} %bitcast.52, f32[1024,128]{1,0:T(8,128)S(1)} %copy.20, f32[]{:T(128)} %constant.6.clone.1), kind=kCustom, calls=%fused_computation.16 | custom fusion | bytes 2097156 | tf_op jit(solution)/shard_map/scatter | solution.py:40
  135.1 5.0 %all-to-all-start.1 = ((f32[32,128,128]{2,1,0:T(8,128)}), f32[32,128,128]{2,1,0:T(8,128)}, u32[]{:S(2)}, u32[]{:S(2)}) async-start(f32[32,128,128]{2,1,0:T(8,128)} %bitcast.41), calls=%async_computation.1 | async-start | bytes 4194304 | tf_op jit(solution)/shard_map/all_to_all | solution.py:47
  140.4 0.3 convert_reduce_fusion
  140.7 48.0 %all-to-all-done.1 = f32[32,128,128]{2,1,0:T(8,128)} async-done(((f32[32,128,128]{2,1,0:T(8,128)}), f32[32,128,128]{2,1,0:T(8,128)}, u32[]{:S(2)}, u32[]{:S(2)}) %all-to-all-start.1) | async-done | bytes 2097184 | tf_op jit(solution)/shard_map/all_to_all | solution.py:47
  188.6 3.5 slice.14
  192.1 3.5 constant_dynamic-slice_fusion
  195.7 2.2 copy.23
  197.8 2.2 copy.24
  200.0 1.0 broadcast_multiply_fusion
  201.0 4.7 %fusion = (bf16[4096,512]{0,1:T(8,128)(2,1)}, bf16[4096,512]{0,1:T(8,128)(2,1)}) fusion(f32[4096,8,64]{0,2,1:T(8,128)S(1)} %broadcast_multiply_fusion), kind=kLoop, calls=%fused_computation.4 | loop fusion | flops 8388608 | bytes 16777216 | tf_op jit(solution)/shard_map/convert_element_type | solution.py:18
  205.8 3.8 %fusion.1 = f32[128,512]{1,0:T(8,128)S(1)} fusion(bf16[4096,512]{0,1:T(8,128)(2,1)} %get-tuple-element.5, f32[4096]{0:T(1024)S(1)} %bitcast.45), kind=kOutput, calls=%fused_computation.11 | convolution fusion | flops 538443776 | bytes 4472832 | tf_op jit(solution)/shard_map/dot_general | solution.py:20
  209.6 2.2 fusion.5
  211.9 58.1 %all-gather.4.cloned.1.call-done = bf16[4096,512]{1,0:T(8,128)(2,1)} async-done(((bf16[128,512]{1,0:T(8,128)(2,1)}), bf16[4096,512]{1,0:T(8,128)(2,1)}) %all-gather.4.cloned.1.call-update) | async-done | bytes 4194320 | tf_op jit(solution)/shard_map/all_gather | solution.py:69
  270.0 4.8 %convolution_multiply_fusion = f32[4096,128]{1,0:T(8,128)} fusion(bf16[4096,512]{1,0:T(8,128)(2,1)} %all-gather.4.cloned.1.call-done, bf16[128,512]{1,0:T(8,128)(2,1)} %fusion.5), kind=kOutput, calls=%fused_computation.5 | convolution fusion | flops 537395200 | bytes 6422528 | tf_op jit(solution)/shard_map/dot_general | solution.py:68
  274.8 95.4 %reduce-scatter.2.cloned.1.call-done = f32[512,128]{1,0:T(8,128)} async-done(((f32[4096,128]{1,0:T(8,128)}), f32[512,128]{1,0:T(8,128)}) %reduce-scatter.2.cloned.1.call-update) | async-done | bytes 262160 | tf_op jit(solution)/shard_map/reduce_scatter | solution.py:76
  (30 shorter events, 1.0 us)
Async XLA Ops:
  6.5 5.6 %copy-start = (bf16[1024,1024]{1,0:T(8,128)(2,1)S(1)}, bf16[1024,1024]{1,0:T(8,128)(2,1)}, u32[]{:S(2)}) copy-start(bf16[1024,1024]{1,0:T(8,128)(2,1)} %param.7) | copy-start | bytes 6291460
  6.5 5.6 %copy-start.2 = (bf16[1024,64]{0,1:T(8,128)(2,1)S(1)}, bf16[1024,64]{0,1:T(8,128)(2,1)}, u32[]{:S(2)}) copy-start(bf16[1024,64]{0,1:T(8,128)(2,1)} %param.9) | copy-start | bytes 393220
  6.5 7.2 %copy-start.3 = (s32[1024,1]{0,1:T(1,128)S(1)}, s32[1024,1]{0,1:T(1,128)}, u32[]{:S(2)}) copy-start(s32[1024,1]{0,1:T(1,128)} %param.10) | copy-start | bytes 12292
  6.5 117.4 %all-gather.6.cloned.1.call-start = ((), (), s32[]{:S(2)}) async-start(), calls=%async_computation.5 | async-start | bytes 4718592 | tf_op jit(solution)/shard_map/all_gather | solution.py:32
  12.1 11.0 %copy-start.4 = (s32[1024]{0:T(1024)S(1)}, s32[1024]{0:T(1024)}, u32[]{:S(2)}) copy-start(s32[1024]{0:T(1024)} %param.11) | copy-start | bytes 12292
  28.2 106.9 %all-to-all-start = ((f32[32,1,128]{2,1,0:T(1,128)}), f32[32,1,128]{2,1,0:T(1,128)S(1)}, u32[]{:S(2)}, u32[]{:S(2)}) async-start(f32[32,1,128]{2,1,0:T(1,128)} %bitcast.6), calls=%async_computation | async-start | bytes 32768 | tf_op jit(solution)/shard_map/all_to_all | solution.py:54
  135.1 53.5 %all-to-all-start.1 = ((f32[32,128,128]{2,1,0:T(8,128)}), f32[32,128,128]{2,1,0:T(8,128)}, u32[]{:S(2)}, u32[]{:S(2)}) async-start(f32[32,128,128]{2,1,0:T(8,128)} %bitcast.41), calls=%async_computation.1 | async-start | bytes 4194304 | tf_op jit(solution)/shard_map/all_to_all | solution.py:47
  140.1 129.9 %all-gather.4.cloned.1.call-start = ((), (), s32[]{:S(2)}) async-start(), calls=%async_computation.3 | async-start | bytes 4325376 | tf_op jit(solution)/shard_map/all_gather | solution.py:69
  205.8 3.9 %copy-start.1 = (bf16[4096,512]{0,1:T(8,128)(2,1)S(1)}, bf16[4096,512]{0,1:T(8,128)(2,1)}, u32[]{:S(2)}) copy-start(bf16[4096,512]{0,1:T(8,128)(2,1)} %get-tuple-element.6) | copy-start | bytes 12582916
  211.8 158.3 %reduce-scatter.2.cloned.1.call-start = ((), (), s32[]{:S(2)}) async-start(), calls=%async_computation.4 | async-start | bytes 2359296 | tf_op jit(solution)/shard_map/reduce_scatter | solution.py:76
Sparse Core Ops, SparseCore 0:
  13.9 110.0 all-gather.5
  212.0 58.0 all-gather.3
  274.9 95.1 reduce-scatter.1
